TPU v7x, 512 devices: a whole 4x4x16 slice. The times are simulated.
512 devices in a mesh: seq: 64 (over z, y_hi, core), mp: 8 (over y_lo, x).
Axes of the slice: x: 4, y: 4 (y_hi: 2, y_lo: 2; y = y_hi * 2 + y_lo), z: 16, core: 2. Of those that a mesh axis runs over, the one named last changes fastest.
Arguments:
- query: bfloat16 [1, 64, 64, 1024], P(None, 'seq', None, 'mp'), may hold values from -6 to 6
- keys: bfloat16 [1, 64, 64, 1024], P(None, 'seq', None, 'mp'), may hold values from -6 to 6
- values: bfloat16 [1, 64, 64, 1024], P(None, 'seq', None, 'mp'), may hold values from -6 to 6
- resid: bfloat16 [1, 64, 64, 1920], P(None, 'seq', 'mp'), may hold values from -4 to 4
- out_weight: bfloat16 [1024, 1920], P('mp'), may hold values from -0.1875 to 0.1875
- norm_gain: float32 [1920], replicated, may hold values from 0.1 to 1.9
- norm_bias: float32 [1920], replicated, may hold values from -3 to 3
- deconv1_weight: bfloat16 [384, 4, 4, 1920], P('mp'), may hold values from -0.0625 to 0.0625
- deconv1_bias: float32 [384], P('mp'), may hold values from -3 to 3
- deconv2_weight: bfloat16 [384, 4, 4, 384], P('mp'), may hold values from -0.15625 to 0.15625
- deconv2_bias: float32 [384], P('mp'), may hold values from -3 to 3
- final_weight: bfloat16 [384, 308], replicated, may hold values from -0.3125 to 0.3125
- final_bias: float32 [308], replicated, may hold values from -3 to 3
Outputs:
- heatmaps: bfloat16 [1, 256, 256, 308], P(None, 'seq', 'mp')
All inputs are finite; a program needn't handle non-finite values.
Results may differ from a plain program's by a relative error of at most 0.012.
Values may be sent and summed in bfloat16 or wider, within the bound.
A program may use at most 64 MiB of HBM per device.

v0:
```python
import jax
import jax.numpy as jnp
from jax import lax
from jax.sharding import PartitionSpec as P

HEAD_DIM = 64
TAP_TABLE = (((1, 1), (0, 3)), ((2, 0), (1, 2)))
EPSILON = 1e-06


def with_halo(array, sides, width):
    for axis, dim in sides:
        size, length = (lax.axis_size(axis), array.shape[dim])
        up = [(i, (i + 1) % size) for i in range(size - 1)]
        down = [(j, i) for i, j in up]
        last = lax.slice_in_dim(array, length - width, length, axis=dim)
        first = lax.slice_in_dim(array, 0, width, axis=dim)
        before = lax.ppermute(last, axis, up)
        after = lax.ppermute(first, axis, down)
        array = jnp.concatenate([before, array, after], axis=dim)
    return array


def tap_product(window, weight, kernel_row, kernel_col):
    tap = weight[:, kernel_row, kernel_col, :]
    return lax.dot_general(
        window, tap, (((3,), (1,)), ((), ())), preferred_element_type=jnp.float32
    )


def half_rows(padded, weight, tap_pairs, first_row, row_count):
    col_count = padded.shape[2] - 2
    halves = []
    for col_parity in range(2):
        summed = None
        for pad_row, kernel_row in tap_pairs:
            for pad_col, kernel_col in TAP_TABLE[col_parity]:
                window = padded[
                    :,
                    first_row + pad_row : first_row + pad_row + row_count,
                    pad_col : pad_col + col_count,
                    :,
                ]
                product = tap_product(window, weight, kernel_row, kernel_col)
                summed = product if summed is None else summed + product
        halves.append(summed)
    stacked = jnp.stack(halves, axis=3)
    return stacked.reshape(stacked.shape[0], row_count, 2 * col_count, stacked.shape[-1])


def upsample(padded, weight, row_count):
    even_rows = half_rows(padded, weight, TAP_TABLE[0], 0, row_count)
    odd_rows = half_rows(padded, weight, TAP_TABLE[1], 0, row_count)
    stacked = jnp.stack([even_rows, odd_rows], axis=2)
    return stacked.reshape(stacked.shape[0], 2 * row_count, stacked.shape[3], stacked.shape[4])


def pad_columns(field):
    return jnp.pad(field, ((0, 0), (0, 0), (1, 1), (0, 0)))


def layer_norm(stream, norm_gain, norm_bias):
    center = jnp.mean(stream, axis=-1, keepdims=True)
    shifted = stream - center
    variance = jnp.mean(shifted * shifted, axis=-1, keepdims=True)
    return (shifted * lax.rsqrt(variance + EPSILON) * norm_gain + norm_bias).astype(jnp.bfloat16)


def local(
    query,
    keys,
    values,
    resid,
    out_weight,
    norm_gain,
    norm_bias,
    deconv1_weight,
    deconv1_bias,
    deconv2_weight,
    deconv2_bias,
    final_weight,
    final_bias,
):
    frame_count, row_count, col_count, feature_width = query.shape
    local_heads = feature_width // HEAD_DIM
    score_scale = HEAD_DIM ** (-0.5)
    query_count = row_count * col_count
    queries = query.reshape(frame_count, query_count, local_heads, HEAD_DIM)
    start_max = jnp.full((frame_count, query_count, local_heads), -1e30, jnp.float32)
    running_max = start_max
    key_piece = lax.all_gather(keys, "seq", axis=1, tiled=True).reshape(
        frame_count, -1, local_heads, HEAD_DIM
    )
    value_piece = lax.all_gather(values, "seq", axis=1, tiled=True).reshape(
        frame_count, -1, local_heads, HEAD_DIM
    )
    scores = (
        jnp.einsum("fqhd,fkhd->fqhk", queries, key_piece, preferred_element_type=jnp.float32)
        * score_scale
    )
    fresh_max = jnp.maximum(running_max, jnp.max(scores, axis=-1))
    exps = jnp.exp(scores - fresh_max[..., None])
    denominator = jnp.sum(exps, axis=-1)
    weighted = jnp.einsum(
        "fqhk,fkhd->fqhd",
        exps.astype(jnp.bfloat16),
        value_piece,
        preferred_element_type=jnp.float32,
    )
    running_max, denominator, weighted = (fresh_max, denominator, weighted)
    attended = (
        (weighted / denominator[..., None])
        .astype(jnp.bfloat16)
        .reshape(frame_count, row_count, col_count, feature_width)
    )
    partial_value = jnp.dot(attended, out_weight, preferred_element_type=jnp.float32)
    summed = lax.psum(partial_value.astype(jnp.bfloat16), "mp").astype(jnp.float32)
    full_resid = lax.all_gather(resid, "mp", axis=2, tiled=True)
    normed = layer_norm(full_resid.astype(jnp.float32) + summed, norm_gain, norm_bias)
    rimmed = with_halo(normed, (("seq", 1),), 1)
    padded = pad_columns(rimmed)
    deconv_one = upsample(padded, deconv1_weight, row_count)
    hidden_one = jnp.maximum(deconv_one + deconv1_bias, 0.0).astype(jnp.bfloat16)
    gathered = lax.all_gather(hidden_one, "mp", axis=3, tiled=True)
    middle = with_halo(gathered, (("seq", 1),), 1)
    deconv_two = upsample(pad_columns(middle), deconv2_weight, 2 * row_count)
    hidden_two = jnp.maximum(deconv_two + deconv2_bias, 0.0).astype(jnp.bfloat16)
    return (
        jnp.dot(
            lax.all_to_all(hidden_two, "mp", split_axis=2, concat_axis=3, tiled=True),
            final_weight,
            preferred_element_type=jnp.float32,
        )
        + final_bias
    ).astype(jnp.bfloat16)


def solution(mesh):
    placed = (
        P(None, "seq", None, "mp"),
        P(None, "seq", None, "mp"),
        P(None, "seq", None, "mp"),
        P(None, "seq", "mp", None),
        P("mp", None),
        P(),
        P(),
        P("mp", None, None, None),
        P("mp"),
        P("mp", None, None, None),
        P("mp"),
        P(),
        P(),
    )
    return jax.shard_map(
        local, mesh=mesh, in_specs=placed, out_specs=P(None, "seq", "mp", None), check_vma=False
    )
```

profile of v0, /device:TPU:113, one launch (start us, length us, event | category | flops | bytes accessed | tf_op | source)
XLA Modules:
  0.0 476.3 jit_solution(8627854209364443066)
XLA Ops:
  6.5 0.7 all-gather.3.cloned.1.call-update
  7.3 0.7 all-gather.5.cloned.1.call-update
  8.1 0.8 reshape.266
  8.9 22.4 %all_gather.12 = bf16[1,1,64,1920]{3,2,1,0:T(8,128)(2,1)S(1)} all-gather(bf16[1,1,8,1920]{3,2,1,0:T(8,128)(2,1)} %param.16), channel_id=1, replica_groups=mesh['seq'=64,'mp'=8] {'mp'}, dimensions={2}, use_global_device_ids=true | all-gather | bytes 276480 | tf_op jit(solution)/shard_map/all_gather | solution.py:118
  31.2 10.4 %fusion.86 = (bf16[48,1,1,1920]{3,2,1,0:T(2,128)(2,1)}, bf16[48,1,1,1920]{3,2,1,0:T(2,128)(2,1)}, bf16[48,1,1,1920]{3,2,1,0:T(2,128)(2,1)}, bf16[48,1,1,1920]{3,...) fusion(bf16[48,4,4,1920]{3,2,1,0:T(4,128)(2,1)} %param.20), kind=kLoop, calls=%fused_computation.163 | loop fusion | bytes 5898240 | tf_op jit(solution)/shard_map/slice | solution.py:25
  41.6 110.5 %all-gather.3.cloned.1.call-done = bf16[1,64,64,128]{3,2,0,1:T(8,128)(2,1)} async-done(((bf16[1,1,64,128]{3,2,0,1:T(8,128)(2,1)}), bf16[1,64,64,128]{3,2,0,1:T(8,128)(2,1)}) %all-gather.3.cloned.1.call-update) | async-done | bytes 1048592 | tf_op jit(solution)/shard_map/all_gather | solution.py:91
  152.2 5.0 %reshape.308 = bf16[4096,2,64]{2,1,0:T(2,128)(2,1)} reshape(bf16[1,64,64,128]{3,2,0,1:T(8,128)(2,1)} %all-gather.3.cloned.1.call-done) | data formatting | bytes 2097152 | tf_op jit(solution)/shard_map/reshape
  157.2 2.5 fusion.89
  159.7 0.4 fusion.5
  160.1 132.0 %all-gather.5.cloned.1.call-done = bf16[1,64,64,128]{3,2,0,1:T(8,128)(2,1)} async-done(((bf16[1,1,64,128]{3,2,0,1:T(8,128)(2,1)}), bf16[1,64,64,128]{3,2,0,1:T(8,128)(2,1)}) %all-gather.5.cloned.1.call-update) | async-done | bytes 1048592 | tf_op jit(solution)/shard_map/all_gather | solution.py:94
  292.1 5.0 %reshape.309 = bf16[4096,2,64]{2,1,0:T(2,128)(2,1)} reshape(bf16[1,64,64,128]{3,2,0,1:T(8,128)(2,1)} %all-gather.5.cloned.1.call-done) | data formatting | bytes 2097152 | tf_op jit(solution)/shard_map/reshape.4
  297.1 2.3 fusion.28
  299.6 0.9 fusion.1
  300.5 1.9 fusion.87
  302.4 80.3 %all-reduce.4.cloned.1.call-done = bf16[1,1,64,1920]{3,2,1,0:T(8,128)(2,1)} async-done(((bf16[1,1,64,1920]{3,2,1,0:T(8,128)(2,1)}), bf16[1,1,64,1920]{3,2,1,0:T(8,128)(2,1)}) %all-reduce.4.cloned.1.call-update) | async-done | bytes 245776 | tf_op jit(solution)/shard_map/psum | solution.py:117
  382.7 1.1 fusion.44
  383.9 1.2 multiply_reduce_fusion
  385.1 1.1 add_convert_fusion
  386.3 11.0 %collective-permute-start = (bf16[1,1,64,1920]{3,2,1,0:T(8,128)(2,1)S(1)}, bf16[1,1,64,1920]{3,2,1,0:T(8,128)(2,1)S(1)}, u32[]{:S(2)}, u32[]{:S(2)}) collective-permute-start(bf16[1,1,64,1920]{3,2,1,0:T(8,128)(2,1)S(1)} %add_convert_fusion), channel_id=1, source_target_pairs={{0,8},{8,16},{16,24},{24,32},{32,40},{40,48},{48,56},{56,64},{64,7... | collective-permute-start | bytes 737288 | tf_op jit(solution)/shard_map/ppermute | solution.py:18
  397.2 1.9 collective-permute-start.1
  399.2 0.2 fusion.58
  399.6 0.7 collective-permute-done
  400.4 8.0 %collective-permute-done.1 = bf16[1,1,64,1920]{3,2,1,0:T(8,128)(2,1)S(1)} collective-permute-done((bf16[1,1,64,1920]{3,2,1,0:T(8,128)(2,1)S(1)}, bf16[1,1,64,1920]{3,2,1,0:T(8,128)(2,1)S(1)}, u32[]{:S(2)}, u32[]{:S(2)}) %collective-permute-start.1) | collective-permute-done | bytes 245792 | tf_op jit(solution)/shard_map/ppermute | solution.py:19
  408.4 0.2 fusion.39
  408.8 0.2 fusion.61
  409.1 0.2 convolution_add_fusion.20
  409.3 0.2 convolution_add_fusion.18
  409.5 0.2 convolution_add_fusion.17
  409.8 0.2 fusion.22
  410.0 0.2 fusion.24
  410.4 1.2 fusion.48
  411.6 1.2 fusion.47
  412.9 0.2 fusion.21
  413.1 1.2 fusion.20
  414.3 0.2 convolution_add_fusion.13
  414.5 0.2 convolution_add_fusion.12
  414.8 0.2 fusion.19
  415.3 22.5 %all_gather.15 = bf16[1,2,128,384]{2,1,0,3:T(2,128)(2,1)S(1)} all-gather(bf16[1,2,128,48]{2,1,0,3:T(2,128)(2,1)S(1)} %copy.252), channel_id=1, replica_groups=mesh['seq'=64,'mp'=8] {'mp'}, dimensions={3}, use_global_device_ids=true | all-gather | bytes 221184 | tf_op jit(solution)/shard_map/all_gather | solution.py:124
  438.2 7.8 %collective-permute-start.2 = (bf16[1,1,128,384]{3,2,1,0:T(8,128)(2,1)S(1)}, bf16[1,1,128,384]{3,2,1,0:T(8,128)(2,1)S(1)}, u32[]{:S(2)}, u32[]{:S(2)}) collective-permute-start(bf16[1,1,128,384]{3,2,1,0:T(8,128)(2,1)S(1)} %get-tuple-element.37), channel_id=1, source_target_pairs={{0,8},{8,16},{16,24},{24,32},{32,40},{40,48},{48,56},{56,64},{64,7... | collective-permute-start | bytes 294920 | tf_op jit(solution)/shard_map/ppermute | solution.py:18
  446.0 1.9 collective-permute-start.3
  448.2 7.4 %collective-permute-done.3 = bf16[1,1,128,384]{3,2,1,0:T(8,128)(2,1)S(1)} collective-permute-done((bf16[1,1,128,384]{3,2,1,0:T(8,128)(2,1)S(1)}, bf16[1,1,128,384]{3,2,1,0:T(8,128)(2,1)S(1)}, u32[]{:S(2)}, u32[]{:S(2)}) %collective-permute-start.3) | collective-permute-done | bytes 98336 | tf_op jit(solution)/shard_map/ppermute | solution.py:19
  456.8 0.2 fusion.16
  457.0 0.2 fusion.18
  457.9 0.2 fusion.15
  459.6 0.4 reshape.310
  460.0 8.2 %all_to_all.15 = bf16[8,2,3072]{2,1,0:T(2,128)(2,1)S(1)} all-to-all(bf16[8,2,3072]{2,1,0:T(2,128)(2,1)S(1)} %reshape.310), channel_id=1, replica_groups=mesh['seq'=64,'mp'=8] {'mp'}, dimensions={0} | all-to-all | bytes 196608 | tf_op jit(solution)/shard_map/all_to_all | solution.py:130
  468.3 0.2 reshape.311
  468.9 0.9 fusion.9
  (119 shorter events, 5.2 us)
Async XLA Ops:
  6.5 293.0 %copy-start = (bf16[128,1920]{1,0:T(8,128)(2,1)S(1)}, bf16[128,1920]{1,0:T(8,128)(2,1)}, u32[]{:S(2)}) copy-start(bf16[128,1920]{1,0:T(8,128)(2,1)} %param.17) | copy-start | bytes 1474564
  6.5 145.7 %all-gather.3.cloned.1.call-start = ((), (), s32[]{:S(2)}) async-start(), calls=%async_computation.1 | async-start | bytes 1064960 | tf_op jit(solution)/shard_map/all_gather | solution.py:91
  7.3 284.9 %all-gather.5.cloned.1.call-start = ((), (), s32[]{:S(2)}) async-start(), calls=%async_computation.2 | async-start | bytes 1064960 | tf_op jit(solution)/shard_map/all_gather | solution.py:94
  8.0 374.7 %all-reduce.4.cloned.1.call-start = ((), (), s32[]{:S(2)}) async-start(), calls=%async_computation.3 | async-start | bytes 491520 | tf_op jit(solution)/shard_map/psum | solution.py:117
  297.1 3.4 copy-start.1
  299.5 85.5 %copy-start.31 = (f32[1920]{0:T(1024)S(1)}, f32[1920]{0:T(1024)}, u32[]{:S(2)}) copy-start(f32[1920]{0:T(1024)} %param.19) | copy-start | bytes 23044
  299.6 85.5 %copy-start.32 = (f32[1920]{0:T(1024)S(1)}, f32[1920]{0:T(1024)}, u32[]{:S(2)}) copy-start(f32[1920]{0:T(1024)} %param.18) | copy-start | bytes 23044
  300.5 98.6 %copy-start.3 = (bf16[48,1,1,1920]{3,2,1,0:T(2,128)(2,1)S(1)}, bf16[48,1,1,1920]{3,2,1,0:T(2,128)(2,1)}, u32[]{:S(2)}) copy-start(bf16[48,1,1,1920]{3,2,1,0:T(2,128)(2,1)} %get-tuple-element.19) | copy-start | bytes 552964
  300.5 98.9 %copy-start.2 = (bf16[48,1,1,1920]{3,2,1,0:T(2,128)(2,1)S(1)}, bf16[48,1,1,1920]{3,2,1,0:T(2,128)(2,1)}, u32[]{:S(2)}) copy-start(bf16[48,1,1,1920]{3,2,1,0:T(2,128)(2,1)} %get-tuple-element.10) | copy-start | bytes 552964
  302.4 106.2 %copy-start.14 = (bf16[48,1,1,1920]{3,2,1,0:T(2,128)(2,1)S(1)}, bf16[48,1,1,1920]{3,2,1,0:T(2,128)(2,1)}, u32[]{:S(2)}) copy-start(bf16[48,1,1,1920]{3,2,1,0:T(2,128)(2,1)} %get-tuple-element.17) | copy-start | bytes 552964
  383.8 25.0 %copy-start.13 = (bf16[48,1,1,1920]{3,2,1,0:T(2,128)(2,1)S(1)}, bf16[48,1,1,1920]{3,2,1,0:T(2,128)(2,1)}, u32[]{:S(2)}) copy-start(bf16[48,1,1,1920]{3,2,1,0:T(2,128)(2,1)} %get-tuple-element.16) | copy-start | bytes 552964
  385.1 23.9 %copy-start.12 = (bf16[48,1,1,1920]{3,2,1,0:T(2,128)(2,1)S(1)}, bf16[48,1,1,1920]{3,2,1,0:T(2,128)(2,1)}, u32[]{:S(2)}) copy-start(bf16[48,1,1,1920]{3,2,1,0:T(2,128)(2,1)} %get-tuple-element.18) | copy-start | bytes 552964
  386.3 14.1 %collective-permute-start = (bf16[1,1,64,1920]{3,2,1,0:T(8,128)(2,1)S(1)}, bf16[1,1,64,1920]{3,2,1,0:T(8,128)(2,1)S(1)}, u32[]{:S(2)}, u32[]{:S(2)}) collective-permute-start(bf16[1,1,64,1920]{3,2,1,0:T(8,128)(2,1)S(1)} %add_convert_fusion), channel_id=1, source_target_pairs={{0,8},{8,16},{16,24},{24,32},{32,40},{40,48},{48,56},{56,64},{64,7... | collective-permute-start | bytes 737288 | tf_op jit(solution)/shard_map/ppermute | solution.py:18
  397.2 11.1 %collective-permute-start.1 = (bf16[1,1,64,1920]{3,2,1,0:T(8,128)(2,1)S(1)}, bf16[1,1,64,1920]{3,2,1,0:T(8,128)(2,1)S(1)}, u32[]{:S(2)}, u32[]{:S(2)}) collective-permute-start(bf16[1,1,64,1920]{3,2,1,0:T(8,128)(2,1)S(1)} %add_convert_fusion), channel_id=1, source_target_pairs={{8,0},{16,8},{24,16},{32,24},{40,32},{48,40},{56,48},{64,56},{72,6... | collective-permute-start | bytes 737288 | tf_op jit(solution)/shard_map/ppermute | solution.py:19
  399.2 10.1 %copy-start.9 = (bf16[48,1,1,1920]{3,2,1,0:T(2,128)(2,1)S(1)}, bf16[48,1,1,1920]{3,2,1,0:T(2,128)(2,1)}, u32[]{:S(2)}) copy-start(bf16[48,1,1,1920]{3,2,1,0:T(2,128)(2,1)} %get-tuple-element.15) | copy-start | bytes 552964
  399.4 10.1 %copy-start.11 = (bf16[48,1,1,1920]{3,2,1,0:T(2,128)(2,1)S(1)}, bf16[48,1,1,1920]{3,2,1,0:T(2,128)(2,1)}, u32[]{:S(2)}) copy-start(bf16[48,1,1,1920]{3,2,1,0:T(2,128)(2,1)} %get-tuple-element.14) | copy-start | bytes 552964
  399.6 10.1 %copy-start.8 = (bf16[48,1,1,1920]{3,2,1,0:T(2,128)(2,1)S(1)}, bf16[48,1,1,1920]{3,2,1,0:T(2,128)(2,1)}, u32[]{:S(2)}) copy-start(bf16[48,1,1,1920]{3,2,1,0:T(2,128)(2,1)} %get-tuple-element.13) | copy-start | bytes 552964
  408.6 1.4 copy-start.7
  409.1 3.8 copy-start.6
  409.5 4.8 copy-start.5
  409.8 4.8 %copy-start.10 = (bf16[48,1,1,1920]{3,2,1,0:T(2,128)(2,1)S(1)}, bf16[48,1,1,1920]{3,2,1,0:T(2,128)(2,1)}, u32[]{:S(2)}) copy-start(bf16[48,1,1,1920]{3,2,1,0:T(2,128)(2,1)} %get-tuple-element.6) | copy-start | bytes 552964
  410.2 4.6 copy-start.4
  410.4 4.8 %copy-start.34 = (f32[48]{0:T(128)S(1)}, f32[48]{0:T(128)}, u32[]{:S(2)}) copy-start(f32[48]{0:T(128)} %param.21) | copy-start | bytes 580
  412.9 25.2 %copy-start.16 = (bf16[48,1,1,384]{3,2,1,0:T(2,128)(2,1)S(1)}, bf16[48,1,1,384]{3,2,1,0:T(2,128)(2,1)}, u32[]{:S(2)}) copy-start(bf16[48,1,1,384]{3,2,1,0:T(2,128)(2,1)} %get-tuple-element.35) | copy-start | bytes 110596
  414.5 41.2 %copy-start.30 = (bf16[48,1,1,384]{3,2,1,0:T(2,128)(2,1)S(1)}, bf16[48,1,1,384]{3,2,1,0:T(2,128)(2,1)}, u32[]{:S(2)}) copy-start(bf16[48,1,1,384]{3,2,1,0:T(2,128)(2,1)} %get-tuple-element.33) | copy-start | bytes 110596
  414.5 41.4 %copy-start.29 = (bf16[48,1,1,384]{3,2,1,0:T(2,128)(2,1)S(1)}, bf16[48,1,1,384]{3,2,1,0:T(2,128)(2,1)}, u32[]{:S(2)}) copy-start(bf16[48,1,1,384]{3,2,1,0:T(2,128)(2,1)} %get-tuple-element.32) | copy-start | bytes 110596
  414.8 41.4 %copy-start.22 = (bf16[48,1,1,384]{3,2,1,0:T(2,128)(2,1)S(1)}, bf16[48,1,1,384]{3,2,1,0:T(2,128)(2,1)}, u32[]{:S(2)}) copy-start(bf16[48,1,1,384]{3,2,1,0:T(2,128)(2,1)} %get-tuple-element.34) | copy-start | bytes 110596
  414.8 41.6 %copy-start.21 = (bf16[48,1,1,384]{3,2,1,0:T(2,128)(2,1)S(1)}, bf16[48,1,1,384]{3,2,1,0:T(2,128)(2,1)}, u32[]{:S(2)}) copy-start(bf16[48,1,1,384]{3,2,1,0:T(2,128)(2,1)} %get-tuple-element.31) | copy-start | bytes 110596
  415.0 41.5 %copy-start.28 = (bf16[48,1,1,384]{3,2,1,0:T(2,128)(2,1)S(1)}, bf16[48,1,1,384]{3,2,1,0:T(2,128)(2,1)}, u32[]{:S(2)}) copy-start(bf16[48,1,1,384]{3,2,1,0:T(2,128)(2,1)} %get-tuple-element.30) | copy-start | bytes 110596
  437.8 19.0 %copy-start.20 = (bf16[48,1,1,384]{3,2,1,0:T(2,128)(2,1)S(1)}, bf16[48,1,1,384]{3,2,1,0:T(2,128)(2,1)}, u32[]{:S(2)}) copy-start(bf16[48,1,1,384]{3,2,1,0:T(2,128)(2,1)} %get-tuple-element.29) | copy-start | bytes 110596
  438.0 19.0 %copy-start.24 = (bf16[48,1,1,384]{3,2,1,0:T(2,128)(2,1)S(1)}, bf16[48,1,1,384]{3,2,1,0:T(2,128)(2,1)}, u32[]{:S(2)}) copy-start(bf16[48,1,1,384]{3,2,1,0:T(2,128)(2,1)} %get-tuple-element.21) | copy-start | bytes 110596
  438.2 9.9 %collective-permute-start.2 = (bf16[1,1,128,384]{3,2,1,0:T(8,128)(2,1)S(1)}, bf16[1,1,128,384]{3,2,1,0:T(8,128)(2,1)S(1)}, u32[]{:S(2)}, u32[]{:S(2)}) collective-permute-start(bf16[1,1,128,384]{3,2,1,0:T(8,128)(2,1)S(1)} %get-tuple-element.37), channel_id=1, source_target_pairs={{0,8},{8,16},{16,24},{24,32},{32,40},{40,48},{48,56},{56,64},{64,7... | collective-permute-start | bytes 294920 | tf_op jit(solution)/shard_map/ppermute | solution.py:18
  446.0 9.5 %collective-permute-start.3 = (bf16[1,1,128,384]{3,2,1,0:T(8,128)(2,1)S(1)}, bf16[1,1,128,384]{3,2,1,0:T(8,128)(2,1)S(1)}, u32[]{:S(2)}, u32[]{:S(2)}) collective-permute-start(bf16[1,1,128,384]{3,2,1,0:T(8,128)(2,1)S(1)} %get-tuple-element.38), channel_id=1, source_target_pairs={{8,0},{16,8},{24,16},{32,24},{40,32},{48,40},{56,48},{64,56},{72,6... | collective-permute-start | bytes 294920 | tf_op jit(solution)/shard_map/ppermute | solution.py:19
  448.1 9.4 %copy-start.27 = (bf16[48,1,1,384]{3,2,1,0:T(2,128)(2,1)S(1)}, bf16[48,1,1,384]{3,2,1,0:T(2,128)(2,1)}, u32[]{:S(2)}) copy-start(bf16[48,1,1,384]{3,2,1,0:T(2,128)(2,1)} %get-tuple-element.27) | copy-start | bytes 110596
  455.7 2.0 copy-start.26
  455.9 2.0 copy-start.23
  456.1 2.0 copy-start.19
  456.3 2.0 copy-start.18
  456.6 2.0 copy-start.25
  456.8 2.0 copy-start.17
  457.5 1.8 copy-start.35
  458.8 10.1 %copy-start.15 = (bf16[384,308]{0,1:T(8,128)(2,1)S(1)}, bf16[384,308]{0,1:T(8,128)(2,1)}, u32[]{:S(2)}) copy-start(bf16[384,308]{0,1:T(8,128)(2,1)} %param.24) | copy-start | bytes 709636
  458.8 10.1 %copy-start.33 = (f32[308]{0:T(512)S(1)}, f32[308]{0:T(512)}, u32[]{:S(2)}) copy-start(f32[308]{0:T(512)} %param.25) | copy-start | bytes 3700
Sparse Core Ops, SparseCore 0:
  10.6 141.5 all-gather.2
  155.5 136.5 all-gather.4
  300.6 82.0 all-reduce.3
where the time goes:
time: 477 us; the launch traced here: 476 us
  waiting for transfers between devices  340 us (71%)
  blocking collectives  53.1 us (11%)
  local copies, waits for them, and re-layouts  25.6 us (5%)
  starting transfers between devices  22.7 us (5%)
  matrix products  16 us (3%)
  between operations  14.1 us (3%)
    all_gather x1, waiting for transfers between devices, local(): lax.all_gather(values, 'seq', axis=1, tiled=True)  132 us
    all_gather x1, waiting for transfers between devices, local(): lax.all_gather(keys, 'seq', axis=1, tiled=True)  111 us
    psum x1, waiting for transfers between devices, local(): lax.psum(partial_value.astype(jnp.bfloat16), 'mp').astype(jnp.float32)  80.3 us
    all_gather x1, blocking collectives, local(): gathered = lax.all_gather(hidden_one, 'mp', axis=3, tiled=True)  22.5 us
    all_gather x1, blocking collectives, local(): full_resid = lax.all_gather(resid, 'mp', axis=2, tiled=True)  22.4 us
    ppermute x2, starting transfers between devices, with_halo(): before = lax.ppermute(last, axis, up)  18.7 us
    ppermute x2, waiting for transfers between devices, with_halo(): after = lax.ppermute(first, axis, down)  15.4 us
    slice x2, local copies, waits for them, and re-layouts, tap_product(): tap = weight[:, kernel_row, kernel_col, :]  12.3 us
  transfers between devices with their start and end apart: 7, of which 6 were waited for; matrix products, arithmetic and copies ran while one was open for 5% of the time, Pallas kernels for 0%

commit v1 on v0

--- a/solution.py
+++ b/solution.py
@@ -114,7 +114,9 @@
         .reshape(frame_count, row_count, col_count, feature_width)
     )
     partial_value = jnp.dot(attended, out_weight, preferred_element_type=jnp.float32)
-    summed = lax.psum(partial_value.astype(jnp.bfloat16), "mp").astype(jnp.float32)
+    summed = jnp.sum(lax.all_gather(partial_value.astype(jnp.bfloat16), "mp"), axis=0).astype(
+        jnp.float32
+    )
     full_resid = lax.all_gather(resid, "mp", axis=2, tiled=True)
     normed = layer_norm(full_resid.astype(jnp.float32) + summed, norm_gain, norm_bias)
     rimmed = with_halo(normed, (("seq", 1),), 1)

time: 477 us -> 435 us (0.912)
  waiting for transfers between devices: 340 us -> 298 us
    psum x1 -> x0, waiting for transfers between devices: 80.3 us -> none  [local(): lax.psum(partial_value.astype(jnp.bfloat16), 'mp').astype(jnp.float32)]
    all_gather x1, waiting for transfers between devices: 111 us -> 143 us  [local(): lax.all_gather(keys, 'seq', axis=1, tiled=True)]
    all_gather x0 -> x1, waiting for transfers between devices: none -> 5.02 us  [local(): lax.all_gather(partial_value.astype(jnp.bfloat16), 'mp')]
where the time goes in v1:
time: 435 us; the launch traced here: 434 us
  waiting for transfers between devices  298 us (69%)
  blocking collectives  56.2 us (13%)
  local copies, waits for them, and re-layouts  23.5 us (5%)
  starting transfers between devices  22.9 us (5%)
  matrix products  16 us (4%)
  between operations  14.1 us (3%)
    all_gather x1, waiting for transfers between devices, local(): lax.all_gather(keys, 'seq', axis=1, tiled=True)  143 us
    all_gather x1, waiting for transfers between devices, local(): lax.all_gather(values, 'seq', axis=1, tiled=True)  132 us
    all_gather x1, blocking collectives, local(): full_resid = lax.all_gather(resid, 'mp', axis=2, tiled=True)  25.9 us
    all_gather x1, blocking collectives, local(): gathered = lax.all_gather(hidden_one, 'mp', axis=3, tiled=True)  22.2 us
    ppermute x2, starting transfers between devices, with_halo(): before = lax.ppermute(last, axis, up)  19 us
    ppermute x2, waiting for transfers between devices, with_halo(): after = lax.ppermute(first, axis, down)  15.4 us
    slice x2, local copies, waits for them, and re-layouts, tap_product(): tap = weight[:, kernel_row, kernel_col, :]  10.2 us
    dot_general x32, matrix products, tap_product(): lax.dot_general(window, tap, (((3,), (1,)), ((), ())), preferred_element_...  9.41 us
  transfers between devices with their start and end apart: 7, of which 6 were waited for; matrix products, arithmetic and copies ran while one was open for 5% of the time, Pallas kernels for 0%

profile of v1, /device:TPU:113, one launch (start us, length us, event | category | flops | bytes accessed | tf_op | source)
XLA Modules:
  0.0 434.1 jit_solution(13974839851902762069)
XLA Ops:
  6.5 0.7 all-gather.5.cloned.1.call-update
  7.3 0.7 all-gather.7.cloned.1.call-update
  8.1 0.8 reshape.278
  8.9 143.3 %all-gather.5.cloned.1.call-done = bf16[1,64,64,128]{3,2,0,1:T(8,128)(2,1)} async-done(((bf16[1,1,64,128]{3,2,0,1:T(8,128)(2,1)}), bf16[1,64,64,128]{3,2,0,1:T(8,128)(2,1)}) %all-gather.5.cloned.1.call-update) | async-done | bytes 1048592 | tf_op jit(solution)/shard_map/all_gather | solution.py:91
  152.2 5.0 %reshape.323 = bf16[4096,2,64]{2,1,0:T(2,128)(2,1)} reshape(bf16[1,64,64,128]{3,2,0,1:T(8,128)(2,1)} %all-gather.5.cloned.1.call-done) | data formatting | bytes 2097152 | tf_op jit(solution)/shard_map/reshape
  157.2 2.5 fusion.88
  159.7 0.4 fusion.4
  160.1 132.0 %all-gather.7.cloned.1.call-done = bf16[1,64,64,128]{3,2,0,1:T(8,128)(2,1)} async-done(((bf16[1,1,64,128]{3,2,0,1:T(8,128)(2,1)}), bf16[1,64,64,128]{3,2,0,1:T(8,128)(2,1)}) %all-gather.7.cloned.1.call-update) | async-done | bytes 1048592 | tf_op jit(solution)/shard_map/all_gather | solution.py:94
  292.1 5.0 %reshape.324 = bf16[4096,2,64]{2,1,0:T(2,128)(2,1)} reshape(bf16[1,64,64,128]{3,2,0,1:T(8,128)(2,1)} %all-gather.7.cloned.1.call-done) | data formatting | bytes 2097152 | tf_op jit(solution)/shard_map/reshape.4
  297.1 2.2 fusion.27
  299.5 0.9 convolution_convert_fusion
  300.5 25.9 %all_gather.18 = bf16[1,1,64,1920]{3,2,1,0:T(8,128)(2,1)} all-gather(bf16[1,1,8,1920]{3,2,1,0:T(8,128)(2,1)S(1)} %copy-done.32), channel_id=1, replica_groups=mesh['seq'=64,'mp'=8] {'mp'}, dimensions={2}, use_global_device_ids=true | all-gather | bytes 276480 | tf_op jit(solution)/shard_map/all_gather | solution.py:120
  326.4 3.8 fusion.86
  330.2 6.4 %fusion.85 = (bf16[48,1,1,1920]{3,2,1,0:T(2,128)(2,1)}, bf16[48,1,1,1920]{3,2,1,0:T(2,128)(2,1)}, bf16[48,1,1,1920]{3,2,1,0:T(2,128)(2,1)}, bf16[48,1,1,1920]{3,...) fusion(bf16[48,4,4,1920]{3,2,1,0:T(4,128)(2,1)S(1)} %copy-done.1), kind=kLoop, calls=%fused_computation.162 | loop fusion | bytes 5898240 | tf_op jit(solution)/shard_map/slice | solution.py:25
  336.7 5.0 %all-gather.9.cloned.1.call-done = bf16[512,1920]{1,0:T(8,128)(2,1)} async-done(((bf16[64,1920]{1,0:T(8,128)(2,1)}), bf16[512,1920]{1,0:T(8,128)(2,1)}) %all-gather.9.cloned.1.call-update) | async-done | bytes 1966096 | tf_op jit(solution)/shard_map/all_gather | solution.py:117
  341.7 1.9 reduce.6
  343.8 0.2 multiply_reduce_fusion
  344.2 10.8 %collective-permute-start = (bf16[1,1,64,1920]{3,2,1,0:T(8,128)(2,1)S(1)}, bf16[1,1,64,1920]{3,2,1,0:T(8,128)(2,1)S(1)}, u32[]{:S(2)}, u32[]{:S(2)}) collective-permute-start(bf16[1,1,64,1920]{3,2,1,0:T(8,128)(2,1)S(1)} %add_convert_fusion), channel_id=1, source_target_pairs={{0,8},{8,16},{16,24},{24,32},{32,40},{40,48},{48,56},{56,64},{64,7... | collective-permute-start | bytes 737288 | tf_op jit(solution)/shard_map/ppermute | solution.py:18
  355.0 1.9 collective-permute-start.1
  357.0 0.2 fusion.57
  357.2 0.2 fusion.54
  357.4 0.7 collective-permute-done
  358.1 8.0 %collective-permute-done.1 = bf16[1,1,64,1920]{3,2,1,0:T(8,128)(2,1)S(1)} collective-permute-done((bf16[1,1,64,1920]{3,2,1,0:T(8,128)(2,1)S(1)}, bf16[1,1,64,1920]{3,2,1,0:T(8,128)(2,1)S(1)}, u32[]{:S(2)}, u32[]{:S(2)}) %collective-permute-start.1) | collective-permute-done | bytes 245792 | tf_op jit(solution)/shard_map/ppermute | solution.py:19
  366.2 0.2 fusion.38
  366.4 0.2 fusion.48
  366.6 0.2 fusion.60
  366.9 0.2 convolution_add_fusion.20
  367.1 0.2 convolution_add_fusion.18
  367.3 0.2 convolution_add_fusion.17
  367.6 0.2 fusion.21
  367.8 0.2 fusion.23
  368.2 1.2 fusion.47
  369.4 1.2 fusion.46
  370.6 0.2 fusion.20
  370.9 1.2 fusion.19
  372.1 0.2 convolution_add_fusion.13
  372.3 0.2 convolution_add_fusion.12
  372.6 0.2 fusion.18
  373.1 22.2 %all_gather.23 = bf16[1,2,128,384]{2,1,0,3:T(2,128)(2,1)S(1)} all-gather(bf16[1,2,128,48]{2,1,0,3:T(2,128)(2,1)S(1)} %copy.252), channel_id=1, replica_groups=mesh['seq'=64,'mp'=8] {'mp'}, dimensions={3}, use_global_device_ids=true | all-gather | bytes 221184 | tf_op jit(solution)/shard_map/all_gather | solution.py:126
  395.7 8.1 %collective-permute-start.2 = (bf16[1,1,128,384]{3,2,1,0:T(8,128)(2,1)S(1)}, bf16[1,1,128,384]{3,2,1,0:T(8,128)(2,1)S(1)}, u32[]{:S(2)}, u32[]{:S(2)}) collective-permute-start(bf16[1,1,128,384]{3,2,1,0:T(8,128)(2,1)S(1)} %get-tuple-element.37), channel_id=1, source_target_pairs={{0,8},{8,16},{16,24},{24,32},{32,40},{40,48},{48,56},{56,64},{64,7... | collective-permute-start | bytes 294920 | tf_op jit(solution)/shard_map/ppermute | solution.py:18
  403.8 1.9 collective-permute-start.3
  406.0 7.4 %collective-permute-done.3 = bf16[1,1,128,384]{3,2,1,0:T(8,128)(2,1)S(1)} collective-permute-done((bf16[1,1,128,384]{3,2,1,0:T(8,128)(2,1)S(1)}, bf16[1,1,128,384]{3,2,1,0:T(8,128)(2,1)S(1)}, u32[]{:S(2)}, u32[]{:S(2)}) %collective-permute-start.3) | collective-permute-done | bytes 98336 | tf_op jit(solution)/shard_map/ppermute | solution.py:19
  414.8 0.2 fusion.17
  415.8 0.2 fusion.14
  417.5 0.4 reshape.325
  417.8 8.1 %all_to_all.15 = bf16[8,2,3072]{2,1,0:T(2,128)(2,1)S(1)} all-to-all(bf16[8,2,3072]{2,1,0:T(2,128)(2,1)S(1)} %reshape.325), channel_id=1, replica_groups=mesh['seq'=64,'mp'=8] {'mp'}, dimensions={0} | all-to-all | bytes 196608 | tf_op jit(solution)/shard_map/all_to_all | solution.py:132
  426.0 0.2 reshape.326
  426.6 0.9 fusion.8
  (124 shorter events, 5.4 us)
Async XLA Ops:
  6.5 293.0 %copy-start = (bf16[128,1920]{1,0:T(8,128)(2,1)S(1)}, bf16[128,1920]{1,0:T(8,128)(2,1)}, u32[]{:S(2)}) copy-start(bf16[128,1920]{1,0:T(8,128)(2,1)} %param.17) | copy-start | bytes 1474564
  6.5 145.7 %all-gather.5.cloned.1.call-start = ((), (), s32[]{:S(2)}) async-start(), calls=%async_computation.1 | async-start | bytes 1064960 | tf_op jit(solution)/shard_map/all_gather | solution.py:91
  7.3 284.9 %all-gather.7.cloned.1.call-start = ((), (), s32[]{:S(2)}) async-start(), calls=%async_computation.2 | async-start | bytes 1064960 | tf_op jit(solution)/shard_map/all_gather | solution.py:94
  8.0 333.7 %all-gather.9.cloned.1.call-start = ((), (), s32[]{:S(2)}) async-start(), calls=%async_computation.3 | async-start | bytes 2211840 | tf_op jit(solution)/shard_map/all_gather | solution.py:117
  297.1 3.4 copy-start.32
  299.4 30.8 %copy-start.1 = (bf16[48,4,4,1920]{3,2,1,0:T(4,128)(2,1)S(1)}, bf16[48,4,4,1920]{3,2,1,0:T(4,128)(2,1)}, u32[]{:S(2)}) copy-start(bf16[48,4,4,1920]{3,2,1,0:T(4,128)(2,1)} %param.20) | copy-start | bytes 8847364
  336.6 6.9 %copy-start.2 = (bf16[1,1,64,1920]{3,2,1,0:T(8,128)(2,1)S(1)}, bf16[1,1,64,1920]{3,2,1,0:T(8,128)(2,1)}, u32[]{:S(2)}) copy-start(bf16[1,1,64,1920]{3,2,1,0:T(8,128)(2,1)} %all_gather.18) | copy-start | bytes 737284
  336.6 7.4 %copy-start.33 = (f32[1920]{0:T(1024)S(1)}, f32[1920]{0:T(1024)}, u32[]{:S(2)}) copy-start(f32[1920]{0:T(1024)} %param.19) | copy-start | bytes 23044
  336.7 7.4 %copy-start.34 = (f32[1920]{0:T(1024)S(1)}, f32[1920]{0:T(1024)}, u32[]{:S(2)}) copy-start(f32[1920]{0:T(1024)} %param.18) | copy-start | bytes 23044
  336.7 20.3 %copy-start.4 = (bf16[48,1,1,1920]{3,2,1,0:T(2,128)(2,1)S(1)}, bf16[48,1,1,1920]{3,2,1,0:T(2,128)(2,1)}, u32[]{:S(2)}) copy-start(bf16[48,1,1,1920]{3,2,1,0:T(2,128)(2,1)} %get-tuple-element.19) | copy-start | bytes 552964
  341.7 15.5 %copy-start.3 = (bf16[48,1,1,1920]{3,2,1,0:T(2,128)(2,1)S(1)}, bf16[48,1,1,1920]{3,2,1,0:T(2,128)(2,1)}, u32[]{:S(2)}) copy-start(bf16[48,1,1,1920]{3,2,1,0:T(2,128)(2,1)} %get-tuple-element.10) | copy-start | bytes 552964
  343.6 22.8 %copy-start.15 = (bf16[48,1,1,1920]{3,2,1,0:T(2,128)(2,1)S(1)}, bf16[48,1,1,1920]{3,2,1,0:T(2,128)(2,1)}, u32[]{:S(2)}) copy-start(bf16[48,1,1,1920]{3,2,1,0:T(2,128)(2,1)} %get-tuple-element.17) | copy-start | bytes 552964
  343.8 22.8 %copy-start.14 = (bf16[48,1,1,1920]{3,2,1,0:T(2,128)(2,1)S(1)}, bf16[48,1,1,1920]{3,2,1,0:T(2,128)(2,1)}, u32[]{:S(2)}) copy-start(bf16[48,1,1,1920]{3,2,1,0:T(2,128)(2,1)} %get-tuple-element.16) | copy-start | bytes 552964
  344.0 22.8 %copy-start.13 = (bf16[48,1,1,1920]{3,2,1,0:T(2,128)(2,1)S(1)}, bf16[48,1,1,1920]{3,2,1,0:T(2,128)(2,1)}, u32[]{:S(2)}) copy-start(bf16[48,1,1,1920]{3,2,1,0:T(2,128)(2,1)} %get-tuple-element.18) | copy-start | bytes 552964
  344.2 13.9 %collective-permute-start = (bf16[1,1,64,1920]{3,2,1,0:T(8,128)(2,1)S(1)}, bf16[1,1,64,1920]{3,2,1,0:T(8,128)(2,1)S(1)}, u32[]{:S(2)}, u32[]{:S(2)}) collective-permute-start(bf16[1,1,64,1920]{3,2,1,0:T(8,128)(2,1)S(1)} %add_convert_fusion), channel_id=1, source_target_pairs={{0,8},{8,16},{16,24},{24,32},{32,40},{40,48},{48,56},{56,64},{64,7... | collective-permute-start | bytes 737288 | tf_op jit(solution)/shard_map/ppermute | solution.py:18
  355.0 11.1 %collective-permute-start.1 = (bf16[1,1,64,1920]{3,2,1,0:T(8,128)(2,1)S(1)}, bf16[1,1,64,1920]{3,2,1,0:T(8,128)(2,1)S(1)}, u32[]{:S(2)}, u32[]{:S(2)}) collective-permute-start(bf16[1,1,64,1920]{3,2,1,0:T(8,128)(2,1)S(1)} %add_convert_fusion), channel_id=1, source_target_pairs={{8,0},{16,8},{24,16},{32,24},{40,32},{48,40},{56,48},{64,56},{72,6... | collective-permute-start | bytes 737288 | tf_op jit(solution)/shard_map/ppermute | solution.py:19
  357.0 10.1 %copy-start.10 = (bf16[48,1,1,1920]{3,2,1,0:T(2,128)(2,1)S(1)}, bf16[48,1,1,1920]{3,2,1,0:T(2,128)(2,1)}, u32[]{:S(2)}) copy-start(bf16[48,1,1,1920]{3,2,1,0:T(2,128)(2,1)} %get-tuple-element.15) | copy-start | bytes 552964
  357.2 10.1 %copy-start.12 = (bf16[48,1,1,1920]{3,2,1,0:T(2,128)(2,1)S(1)}, bf16[48,1,1,1920]{3,2,1,0:T(2,128)(2,1)}, u32[]{:S(2)}) copy-start(bf16[48,1,1,1920]{3,2,1,0:T(2,128)(2,1)} %get-tuple-element.14) | copy-start | bytes 552964
  357.4 10.1 %copy-start.9 = (bf16[48,1,1,1920]{3,2,1,0:T(2,128)(2,1)S(1)}, bf16[48,1,1,1920]{3,2,1,0:T(2,128)(2,1)}, u32[]{:S(2)}) copy-start(bf16[48,1,1,1920]{3,2,1,0:T(2,128)(2,1)} %get-tuple-element.13) | copy-start | bytes 552964
  366.4 1.4 copy-start.8
  366.8 3.8 copy-start.7
  367.3 4.8 %copy-start.6 = (bf16[48,1,1,1920]{3,2,1,0:T(2,128)(2,1)S(1)}, bf16[48,1,1,1920]{3,2,1,0:T(2,128)(2,1)}, u32[]{:S(2)}) copy-start(bf16[48,1,1,1920]{3,2,1,0:T(2,128)(2,1)} %get-tuple-element.7) | copy-start | bytes 552964
  367.5 4.8 %copy-start.11 = (bf16[48,1,1,1920]{3,2,1,0:T(2,128)(2,1)S(1)}, bf16[48,1,1,1920]{3,2,1,0:T(2,128)(2,1)}, u32[]{:S(2)}) copy-start(bf16[48,1,1,1920]{3,2,1,0:T(2,128)(2,1)} %get-tuple-element.6) | copy-start | bytes 552964
  368.0 4.6 %copy-start.5 = (bf16[48,1,1,1920]{3,2,1,0:T(2,128)(2,1)S(1)}, bf16[48,1,1,1920]{3,2,1,0:T(2,128)(2,1)}, u32[]{:S(2)}) copy-start(bf16[48,1,1,1920]{3,2,1,0:T(2,128)(2,1)} %get-tuple-element.20) | copy-start | bytes 552964
  368.2 4.8 %copy-start.36 = (f32[48]{0:T(128)S(1)}, f32[48]{0:T(128)}, u32[]{:S(2)}) copy-start(f32[48]{0:T(128)} %param.21) | copy-start | bytes 580
  370.6 24.8 %copy-start.17 = (bf16[48,1,1,384]{3,2,1,0:T(2,128)(2,1)S(1)}, bf16[48,1,1,384]{3,2,1,0:T(2,128)(2,1)}, u32[]{:S(2)}) copy-start(bf16[48,1,1,384]{3,2,1,0:T(2,128)(2,1)} %get-tuple-element.35) | copy-start | bytes 110596
  372.3 41.2 %copy-start.31 = (bf16[48,1,1,384]{3,2,1,0:T(2,128)(2,1)S(1)}, bf16[48,1,1,384]{3,2,1,0:T(2,128)(2,1)}, u32[]{:S(2)}) copy-start(bf16[48,1,1,384]{3,2,1,0:T(2,128)(2,1)} %get-tuple-element.33) | copy-start | bytes 110596
  372.3 41.4 %copy-start.30 = (bf16[48,1,1,384]{3,2,1,0:T(2,128)(2,1)S(1)}, bf16[48,1,1,384]{3,2,1,0:T(2,128)(2,1)}, u32[]{:S(2)}) copy-start(bf16[48,1,1,384]{3,2,1,0:T(2,128)(2,1)} %get-tuple-element.32) | copy-start | bytes 110596
  372.5 41.4 %copy-start.23 = (bf16[48,1,1,384]{3,2,1,0:T(2,128)(2,1)S(1)}, bf16[48,1,1,384]{3,2,1,0:T(2,128)(2,1)}, u32[]{:S(2)}) copy-start(bf16[48,1,1,384]{3,2,1,0:T(2,128)(2,1)} %get-tuple-element.34) | copy-start | bytes 110596
  372.6 41.6 %copy-start.22 = (bf16[48,1,1,384]{3,2,1,0:T(2,128)(2,1)S(1)}, bf16[48,1,1,384]{3,2,1,0:T(2,128)(2,1)}, u32[]{:S(2)}) copy-start(bf16[48,1,1,384]{3,2,1,0:T(2,128)(2,1)} %get-tuple-element.31) | copy-start | bytes 110596
  372.8 41.6 %copy-start.29 = (bf16[48,1,1,384]{3,2,1,0:T(2,128)(2,1)S(1)}, bf16[48,1,1,384]{3,2,1,0:T(2,128)(2,1)}, u32[]{:S(2)}) copy-start(bf16[48,1,1,384]{3,2,1,0:T(2,128)(2,1)} %get-tuple-element.30) | copy-start | bytes 110596
  395.3 19.4 %copy-start.21 = (bf16[48,1,1,384]{3,2,1,0:T(2,128)(2,1)S(1)}, bf16[48,1,1,384]{3,2,1,0:T(2,128)(2,1)}, u32[]{:S(2)}) copy-start(bf16[48,1,1,384]{3,2,1,0:T(2,128)(2,1)} %get-tuple-element.29) | copy-start | bytes 110596
  395.4 19.4 %copy-start.25 = (bf16[48,1,1,384]{3,2,1,0:T(2,128)(2,1)S(1)}, bf16[48,1,1,384]{3,2,1,0:T(2,128)(2,1)}, u32[]{:S(2)}) copy-start(bf16[48,1,1,384]{3,2,1,0:T(2,128)(2,1)} %get-tuple-element.21) | copy-start | bytes 110596
  395.7 10.3 %collective-permute-start.2 = (bf16[1,1,128,384]{3,2,1,0:T(8,128)(2,1)S(1)}, bf16[1,1,128,384]{3,2,1,0:T(8,128)(2,1)S(1)}, u32[]{:S(2)}, u32[]{:S(2)}) collective-permute-start(bf16[1,1,128,384]{3,2,1,0:T(8,128)(2,1)S(1)} %get-tuple-element.37), channel_id=1, source_target_pairs={{0,8},{8,16},{16,24},{24,32},{32,40},{40,48},{48,56},{56,64},{64,7... | collective-permute-start | bytes 294920 | tf_op jit(solution)/shard_map/ppermute | solution.py:18
  403.8 9.5 %collective-permute-start.3 = (bf16[1,1,128,384]{3,2,1,0:T(8,128)(2,1)S(1)}, bf16[1,1,128,384]{3,2,1,0:T(8,128)(2,1)S(1)}, u32[]{:S(2)}, u32[]{:S(2)}) collective-permute-start(bf16[1,1,128,384]{3,2,1,0:T(8,128)(2,1)S(1)} %get-tuple-element.38), channel_id=1, source_target_pairs={{8,0},{16,8},{24,16},{32,24},{40,32},{48,40},{56,48},{64,56},{72,6... | collective-permute-start | bytes 294920 | tf_op jit(solution)/shard_map/ppermute | solution.py:19
  406.0 9.4 %copy-start.28 = (bf16[48,1,1,384]{3,2,1,0:T(2,128)(2,1)S(1)}, bf16[48,1,1,384]{3,2,1,0:T(2,128)(2,1)}, u32[]{:S(2)}) copy-start(bf16[48,1,1,384]{3,2,1,0:T(2,128)(2,1)} %get-tuple-element.27) | copy-start | bytes 110596
  413.5 2.0 copy-start.27
  413.7 2.0 copy-start.24
  414.0 2.0 copy-start.20
  414.2 2.0 copy-start.19
  414.4 2.0 copy-start.26
  414.6 2.0 copy-start.18
  415.3 1.8 copy-start.37
  416.6 10.0 %copy-start.16 = (bf16[384,308]{0,1:T(8,128)(2,1)S(1)}, bf16[384,308]{0,1:T(8,128)(2,1)}, u32[]{:S(2)}) copy-start(bf16[384,308]{0,1:T(8,128)(2,1)} %param.24) | copy-start | bytes 709636
  416.6 10.0 %copy-start.35 = (f32[308]{0:T(512)S(1)}, f32[308]{0:T(512)}, u32[]{:S(2)}) copy-start(f32[308]{0:T(512)} %param.25) | copy-start | bytes 3700
Sparse Core Ops, SparseCore 0:
  10.6 141.5 all-gather.4
  155.5 136.5 all-gather.6
  300.6 41.0 all-gather.8
